TPU v7x, 512 devices: a whole 4x4x16 slice. The times are simulated.
512 devices in a mesh: dp: 32 (over y, x, core), table: 16 (over z).
Axes of the slice: x: 4, y: 4, z: 16, core: 2. Of those that a mesh axis runs over, the one named last changes fastest.
Arguments:
- hidden_in: bfloat16 [4096, 4096], P('dp', 'table'), may hold values from -6 to 6
- gate_weight: bfloat16 [4096, 4096], P('dp', 'table'), may hold values from -0.09375 to 0.09375
- values: bfloat16 [2048, 4096], P('table'), may hold values from -6 to 6
- pick_rows: int32 [4096, 32], P('dp'), may hold values from 0 to 2047, all different within a row
- pick_scores: float32 [4096, 32], P('dp'), may hold values from -300 to 300
- grad_out: bfloat16 [4096, 4096], P('dp', 'table'), may hold values from -6 to 6
Outputs:
- branch_out: bfloat16 [4096, 4096], P('dp', 'table')
- grad_hidden: bfloat16 [4096, 4096], P('dp', 'table')
- grad_gate: float32 [4096, 4096], P('dp', 'table')
- grad_values: float32 [2048, 4096], P('table')
- grad_scores: float32 [4096, 32], P('dp')
Inputs may be any that keep to these rules, and one draw needn't show every extreme that they name: `pick_rows`: the 32 rows of a token are distinct.
All inputs are finite; a program needn't handle non-finite values.
Results may differ from a plain program's by a relative error of at most 0.025.
Values may be sent and summed in bfloat16 or wider, within the bound.
A program may use at most 64 MiB of HBM per device.

v0:
```python
import jax
import jax.numpy as jnp
from jax import lax
from jax.sharding import PartitionSpec as P


def pick_weights(pick_scores):
    row_max = jnp.max(pick_scores, axis=1, keepdims=True)
    exponent = jnp.exp(pick_scores - row_max)
    return exponent / jnp.sum(exponent, axis=1, keepdims=True)


def spread_weights(row_ids, weights_bf, row_total):
    token_ids = lax.broadcasted_iota(jnp.int32, row_ids.shape, 0)
    empty = jnp.zeros((row_ids.shape[0], row_total), jnp.bfloat16)
    return empty.at[token_ids, row_ids].set(weights_bf, mode="drop")


def local(hidden_in, gate_weight, values, pick_rows, pick_scores, grad_out):
    weights = pick_weights(pick_scores)
    weights_bf = weights.astype(jnp.bfloat16)
    token_count = hidden_in.shape[0]
    col_count = hidden_in.shape[1]
    rows_here = values.shape[0]
    whole_in = lax.all_gather(hidden_in, "table", axis=1, tiled=True)
    weight_full = lax.all_gather(gate_weight, "dp", axis=0, tiled=True)
    local_rows = pick_rows - lax.axis_index("table") * rows_here
    owned = (local_rows >= 0) & (local_rows < rows_here)
    parked = jnp.where(owned, local_rows, rows_here)
    spread = spread_weights(parked, weights_bf, rows_here)
    partial_mem = jnp.dot(spread, values, preferred_element_type=jnp.float32)
    arrived = lax.all_to_all(
        partial_mem.astype(jnp.bfloat16), "table", split_axis=1, concat_axis=0, tiled=True
    ).astype(partial_mem.dtype)
    memory_read = jnp.sum(arrived.reshape(-1, token_count, col_count), axis=0)
    gate_input = jnp.dot(whole_in, weight_full, preferred_element_type=jnp.float32)
    sigmoid_v = jax.nn.sigmoid(gate_input)
    gate_value = gate_input * sigmoid_v
    gate_slope = sigmoid_v * (1.0 + gate_input * (1.0 - sigmoid_v))
    branch_out = (memory_read * gate_value).astype(jnp.bfloat16)
    upstream = grad_out.astype(jnp.float32)
    mem_grad = (upstream * gate_value).astype(jnp.bfloat16)
    gate_grad_in = (upstream * memory_read * gate_slope).astype(jnp.bfloat16)
    grad_full = lax.all_gather(mem_grad, "table", axis=1, tiled=True)
    value_term = lax.dot_general(
        spread, grad_full, (((0,), (0,)), ((), ())), preferred_element_type=jnp.float32
    )
    affinity_all = lax.dot_general(
        grad_full, values, (((1,), (1,)), ((), ())), preferred_element_type=jnp.float32
    )
    picked = jnp.take_along_axis(affinity_all, jnp.where(owned, local_rows, 0), axis=1)
    affinity_part = jnp.where(owned, picked, 0.0)
    affinity = lax.psum(affinity_part, "table")
    grad_scores = weights * (affinity - jnp.sum(weights * affinity, axis=1, keepdims=True))
    grad_values = lax.psum(value_term.astype(jnp.bfloat16), "dp").astype(jnp.float32)
    grad_gate = lax.psum_scatter(
        lax.dot_general(
            whole_in, gate_grad_in, (((0,), (0,)), ((), ())), preferred_element_type=jnp.float32
        ).astype(jnp.bfloat16),
        "dp",
        scatter_dimension=0,
        tiled=True,
    ).astype(jnp.float32)
    input_term = lax.dot_general(
        gate_grad_in, weight_full, (((1,), (1,)), ((), ())), preferred_element_type=jnp.float32
    )
    grad_hidden = lax.psum_scatter(
        input_term.astype(jnp.bfloat16), "table", scatter_dimension=1, tiled=True
    )
    return (branch_out, grad_hidden, grad_gate, grad_values, grad_scores)


def solution(mesh):
    placed = (
        P("dp", "table"),
        P("dp", "table"),
        P("table", None),
        P("dp", None),
        P("dp", None),
        P("dp", "table"),
    )
    return jax.shard_map(
        local,
        mesh=mesh,
        in_specs=placed,
        out_specs=(
            P("dp", "table"),
            P("dp", "table"),
            P("dp", "table"),
            P("table", None),
            P("dp", None),
        ),
        check_vma=False,
    )
```

profile of v0, /device:TPU:6, one launch (start us, length us, event | category | flops | bytes accessed | tf_op | source)
XLA Modules:
  0.0 570.6 jit_solution(2590282525393934483)
XLA Ops:
  7.9 0.8 copy.22
  8.9 0.7 multiply_reduce_fusion.1
  9.8 0.8 copy.25
  10.6 0.7 reduce_max.9
  11.7 28.6 %scatter_custom_fusion = bf16[16384]{0:T(1024)(128)(2,1)S(1)} fusion(s32[4096]{0:T(1024)S(1)} %reshape.49, bf16[4096]{0:T(1024)(128)(2,1)S(1)} %reshape.51, bf16[]{:T(256)} %constant.9.clone.1), kind=kCustom, calls=%fused_computation.33 | custom fusion | bytes 32770
  40.8 1.1 copy.33
  41.9 15.3 %all-to-all-start = ((bf16[128,16,256]{2,0,1:T(8,128)(2,1)}), bf16[128,16,256]{2,0,1:T(8,128)(2,1)S(1)}, u32[]{:S(2)}, u32[]{:S(2)}) async-start(bf16[128,16,256]{2,0,1:T(8,128)(2,1)} %bitcast.27), calls=%async_computation | async-start | bytes 2097152 | tf_op jit(solution)/shard_map/all_to_all | solution.py:32
  58.0 54.4 %all-to-all-done = bf16[128,16,256]{2,0,1:T(8,128)(2,1)S(1)} async-done(((bf16[128,16,256]{2,0,1:T(8,128)(2,1)}), bf16[128,16,256]{2,0,1:T(8,128)(2,1)S(1)}, u32[]{:S(2)}, u32[]{:S(2)}) %all-to-all-start) | async-done | bytes 1048608 | tf_op jit(solution)/shard_map/all_to_all | solution.py:32
  112.5 1.2 all-gather.4.cloned.1.call-done
  113.8 59.5 %all-gather.6.cloned.1.call-done = bf16[4096,256]{1,0:T(8,128)(2,1)} async-done(((bf16[128,256]{1,0:T(8,128)(2,1)}), bf16[4096,256]{1,0:T(8,128)(2,1)}) %all-gather.6.cloned.1.call-update) | async-done | bytes 2097168 | tf_op jit(solution)/shard_map/all_gather | solution.py:26
  173.3 3.1 fusion.2
  176.4 72.2 %all-gather.8.cloned.1.call-done = bf16[128,4096]{1,0:T(8,128)(2,1)} async-done(((bf16[128,256]{1,0:T(8,128)(2,1)}), bf16[128,4096]{1,0:T(8,128)(2,1)}) %all-gather.8.cloned.1.call-update) | async-done | bytes 1048592 | tf_op jit(solution)/shard_map/all_gather | solution.py:44
  248.6 2.7 convolution_convert_fusion.1
  251.3 1.9 fusion
  253.3 2.5 copy.29
  255.8 3.5 convolution_convert_fusion.2
  259.9 25.6 %gather_fusion = f32[4096]{0:T(1024)S(1)} fusion(f32[128,128]{1,0:T(8,128)S(1)} %fusion.13, s32[4096]{0:T(1024)S(1)} %reshape.43), kind=kCustom, calls=%fused_computation | custom fusion | bytes 65536 | tf_op jit(solution)/shard_map/jit(take_along_axis)/gather | solution.py:51
  285.7 54.5 %psum.15 = f32[128,32]{1,0:T(8,128)S(1)} all-reduce(f32[128,32]{1,0:T(8,128)S(1)} %select_select_fusion), channel_id=1, replica_groups=mesh['dp'=32,'table'=16] {'table'}, use_global_device_ids=true, to_apply=%region_7.8 | all-reduce | flops 4096 | bytes 32768 | tf_op jit(solution)/shard_map/psum | solution.py:53
  341.2 43.4 %all-reduce.2.cloned.1.call-done = bf16[128,4096]{1,0:T(8,128)(2,1)} async-done(((bf16[128,4096]{1,0:T(8,128)(2,1)}), bf16[128,4096]{1,0:T(8,128)(2,1)}) %all-reduce.2.cloned.1.call-update) | async-done | bytes 1048592 | tf_op jit(solution)/shard_map/psum | solution.py:55
  384.5 2.8 convert_element_type.53
  387.3 102.8 %reduce-scatter.7.cloned.1.call-done = bf16[128,256]{1,0:T(8,128)(2,1)} async-done(((bf16[4096,256]{1,0:T(8,128)(2,1)}), bf16[128,256]{1,0:T(8,128)(2,1)}) %reduce-scatter.7.cloned.1.call-update) | async-done | bytes 65552
  490.1 0.9 copy.30
  491.0 0.8 copy.27
  491.8 72.0 %reduce-scatter.5.cloned.1.call-done = bf16[128,256]{1,0:T(8,128)(2,1)} async-done(((bf16[128,4096]{1,0:T(8,128)(2,1)}), bf16[128,256]{1,0:T(8,128)(2,1)}) %reduce-scatter.5.cloned.1.call-update) | async-done | bytes 65552 | tf_op jit(solution)/shard_map/reduce_scatter | solution.py:67
  (38 shorter events, 4.6 us)
Async XLA Ops:
  7.2 33.2 %copy-start = (bf16[128,4096]{1,0:T(8,128)(2,1)S(1)}, bf16[128,4096]{1,0:T(8,128)(2,1)}, u32[]{:S(2)}) copy-start(bf16[128,4096]{1,0:T(8,128)(2,1)} %param.8) | copy-start | bytes 3145732
  7.2 106.6 %all-gather.4.cloned.1.call-start = ((), (), s32[]{:S(2)}) async-start(), calls=%async_computation.3 | async-start | bytes 1114112 | tf_op jit(solution)/shard_map/all_gather | solution.py:25
  41.9 131.4 %copy-start.2 = (bf16[128,256]{1,0:T(8,128)(2,1)S(1)}, bf16[128,256]{1,0:T(8,128)(2,1)}, u32[]{:S(2)}) copy-start(bf16[128,256]{1,0:T(8,128)(2,1)} %param.11) | copy-start | bytes 196612
  41.9 70.5 %all-to-all-start = ((bf16[128,16,256]{2,0,1:T(8,128)(2,1)}), bf16[128,16,256]{2,0,1:T(8,128)(2,1)S(1)}, u32[]{:S(2)}, u32[]{:S(2)}) async-start(bf16[128,16,256]{2,0,1:T(8,128)(2,1)} %bitcast.27), calls=%async_computation | async-start | bytes 2097152 | tf_op jit(solution)/shard_map/all_to_all | solution.py:32
  57.2 116.1 %all-gather.6.cloned.1.call-start = ((), (), s32[]{:S(2)}) async-start(), calls=%async_computation.4 | async-start | bytes 2162688 | tf_op jit(solution)/shard_map/all_gather | solution.py:26
  58.0 190.6 %all-gather.8.cloned.1.call-start = ((), (), s32[]{:S(2)}) async-start(), calls=%async_computation.6 | async-start | bytes 1114112 | tf_op jit(solution)/shard_map/all_gather | solution.py:44
  176.4 208.2 %all-reduce.2.cloned.1.call-start = ((), (), s32[]{:S(2)}) async-start(), calls=%async_computation.7 | async-start | bytes 2097152 | tf_op jit(solution)/shard_map/psum | solution.py:55
  251.3 238.8 %reduce-scatter.7.cloned.1.call-start = ((), (), s32[]{:S(2)}) async-start(), calls=%async_computation.8 | async-start | bytes 2162688
  255.8 3.7 copy-start.1
  255.8 308.0 %reduce-scatter.5.cloned.1.call-start = ((), (), s32[]{:S(2)}) async-start(), calls=%async_computation.5 | async-start | bytes 1114112 | tf_op jit(solution)/shard_map/reduce_scatter | solution.py:67
Sparse Core Ops, SparseCore 0:
  10.0 103.7 all-gather.3
  116.9 56.3 all-gather.5
  176.5 72.0 all-gather.7
  252.2 132.2 all-reduce.1
  389.4 100.6 reduce-scatter.6
  493.6 70.2 reduce-scatter.4
where the time goes:
time: 571 us
  waiting for transfers between devices  407 us (71%)
  local copies, waits for them, and re-layouts  62.3 us (11%)
  blocking collectives  54.5 us (10%)
  starting transfers between devices  15.6 us (3%)
  between operations  14.3 us (3%)
  matrix products  12 us (2%)
    unnamed x7, waiting for transfers between devices  104 us
    all_gather x1, waiting for transfers between devices, local(): grad_full = lax.all_gather(mem_grad, 'table', axis=1, tiled=True)  72.2 us
    reduce_scatter x1, waiting for transfers between devices, local(): lax.psum_scatter(input_term.astype(jnp.bfloat16), 'table', scatter_dimens...  72 us
    all_gather x1, waiting for transfers between devices, local(): weight_full = lax.all_gather(gate_weight, 'dp', axis=0, tiled=True)  59.5 us
    psum x1, blocking collectives, local(): affinity = lax.psum(affinity_part, 'table')  54.5 us
    all_to_all x1, waiting for transfers between devices, local(): lax.all_to_all(partial_mem.astype(jnp.bfloat16), 'table', split_axis=1, c...  54.4 us
    psum x1, waiting for transfers between devices, local(): lax.psum(value_term.astype(jnp.bfloat16), 'dp').astype(jnp.float32)  43.4 us
    unnamed x15, local copies, waits for them, and re-layouts  35.3 us
  transfers between devices with their start and end apart: 7, of which 7 were waited for; matrix products, arithmetic and copies ran while one was open for 13% of the time, Pallas kernels for 0%

commit v1 on v0

--- a/solution.py
+++ b/solution.py
@@ -2,6 +2,27 @@
 import jax.numpy as jnp
 from jax import lax
 from jax.sharding import PartitionSpec as P
+
+
+def ring_gather(x, axis, dim):
+    peers, index, span = (lax.axis_size(axis), lax.axis_index(axis), x.shape[dim])
+    right = [(i, (i + 1) % peers) for i in range(peers)]
+    left = [(i, (i - 1) % peers) for i in range(peers)]
+    result = jnp.zeros((*x.shape[:dim], peers * span, *x.shape[dim + 1 :]), x.dtype)
+    result = lax.dynamic_update_slice_in_dim(result, x, index * span, axis=dim)
+    from_left = from_right = x
+    halfway = peers // 2
+    for hop in range(1, halfway + 1):
+        from_left = lax.ppermute(from_left, axis, right)
+        result = lax.dynamic_update_slice_in_dim(
+            result, from_left, (index - hop) % peers * span, axis=dim
+        )
+        if hop < peers - halfway:
+            from_right = lax.ppermute(from_right, axis, left)
+            result = lax.dynamic_update_slice_in_dim(
+                result, from_right, (index + hop) % peers * span, axis=dim
+            )
+    return result
 
 
 def pick_weights(pick_scores):
@@ -41,7 +62,7 @@
     upstream = grad_out.astype(jnp.float32)
     mem_grad = (upstream * gate_value).astype(jnp.bfloat16)
     gate_grad_in = (upstream * memory_read * gate_slope).astype(jnp.bfloat16)
-    grad_full = lax.all_gather(mem_grad, "table", axis=1, tiled=True)
+    grad_full = ring_gather(mem_grad, "table", 1)
     value_term = lax.dot_general(
         spread, grad_full, (((0,), (0,)), ((), ())), preferred_element_type=jnp.float32
     )

time: 571 us -> 654 us (1.15)
  starting transfers between devices: 15.6 us -> 62.6 us
  waiting for transfers between devices: 407 us -> 445 us
    all_gather x1, waiting for transfers between devices: 1.23 us -> 74.2 us  [local(): whole_in = lax.all_gather(hidden_in, 'table', axis=1, tiled=True)]
    all_gather x1 -> x0, waiting for transfers between devices: 72.2 us -> none  [local(): grad_full = lax.all_gather(mem_grad, 'table', axis=1, tiled=True)]
    psum x1, waiting for transfers between devices: 43.4 us -> 97.7 us  [local(): lax.psum(value_term.astype(jnp.bfloat16), 'dp').astype(jnp.float32)]
    ppermute x0 -> x15, starting transfers between devices: none -> 52 us  [the longest x7 35.2 us: ring_gather(): from_right = lax.ppermute(from_right, axis, left)]
    all_to_all x1, waiting for transfers between devices: 54.4 us -> 31.6 us  [local(): lax.all_to_all(partial_mem.astype(jnp.bfloat16), 'table', split_axis=1, c...]
    ppermute x0 -> x15, waiting for transfers between devices: none -> 7.29 us  [the longest x8 7.27 us: ring_gather(): from_left = lax.ppermute(from_left, axis, right)]
    unnamed x7 -> x6, waiting for transfers between devices: 104 us -> 104 us
  transfers between devices with their start and end apart: 7 -> 21, of which waited for: 7 -> 14; matrix products, arithmetic and copies ran while one was open for 13% -> 3% of each run, Pallas kernels for 0% -> 0%
where the time goes in v1:
time: 654 us
  waiting for transfers between devices  445 us (68%)
  local copies, waits for them, and re-layouts  64.1 us (10%)
  starting transfers between devices  62.6 us (10%)
  blocking collectives  53.5 us (8%)
  between operations  14.6 us (2%)
  matrix products  8.43 us (1%)
    unnamed x6, waiting for transfers between devices  104 us
    psum x1, waiting for transfers between devices, local(): lax.psum(value_term.astype(jnp.bfloat16), 'dp').astype(jnp.float32)  97.7 us
    all_gather x1, waiting for transfers between devices, local(): whole_in = lax.all_gather(hidden_in, 'table', axis=1, tiled=True)  74.2 us
    reduce_scatter x1, waiting for transfers between devices, local(): lax.psum_scatter(input_term.astype(jnp.bfloat16), 'table', scatter_dimens...  72 us
    all_gather x1, waiting for transfers between devices, local(): weight_full = lax.all_gather(gate_weight, 'dp', axis=0, tiled=True)  57.7 us
    psum x1, blocking collectives, local(): affinity = lax.psum(affinity_part, 'table')  53.5 us
    unnamed x15, local copies, waits for them, and re-layouts  36.8 us
    ppermute x7, starting transfers between devices, ring_gather(): from_right = lax.ppermute(from_right, axis, left)  35.2 us
  transfers between devices with their start and end apart: 21, of which 14 were waited for; matrix products, arithmetic and copies ran while one was open for 3% of the time, Pallas kernels for 0%

profile of v1, /device:TPU:6, one launch (start us, length us, event | category | flops | bytes accessed | tf_op | source)
XLA Modules:
  0.0 653.5 jit_solution(14077035180981401080)
XLA Ops:
  12.6 74.2 %all-gather.3.cloned.1.call-done = bf16[128,4096]{1,0:T(8,128)(2,1)} async-done(((bf16[128,256]{1,0:T(8,128)(2,1)}), bf16[128,4096]{1,0:T(8,128)(2,1)}) %all-gather.3.cloned.1.call-update) | async-done | bytes 1048592 | tf_op jit(solution)/shard_map/all_gather | solution.py:46
  86.7 57.7 %all-gather.5.cloned.1.call-done = bf16[4096,256]{1,0:T(8,128)(2,1)} async-done(((bf16[128,256]{1,0:T(8,128)(2,1)}), bf16[4096,256]{1,0:T(8,128)(2,1)}) %all-gather.5.cloned.1.call-update) | async-done | bytes 2097168 | tf_op jit(solution)/shard_map/all_gather | solution.py:47
  144.6 2.4 constant_dynamic-update-slice_fusion.15
  147.0 3.5 collective-permute-start
  150.4 4.4 collective-permute-start.1
  155.4 1.9 collective-permute-start.2
  157.3 5.1 collective-permute-start.3
  164.7 5.1 collective-permute-start.5
  172.1 5.1 collective-permute-start.7
  179.4 5.1 collective-permute-start.9
  186.8 5.1 collective-permute-start.11
  194.1 5.1 collective-permute-start.13
  201.5 5.4 collective-permute-done.14
  207.4 25.6 %gather_fusion = f32[4096]{0:T(1024)S(1)} fusion(f32[128,128]{1,0:T(8,128)S(1)} %fusion.14, s32[4096]{0:T(1024)S(1)} %reshape.43), kind=kCustom, calls=%fused_computation | custom fusion | bytes 65536 | tf_op jit(solution)/shard_map/jit(take_along_axis)/gather | solution.py:72
  233.1 53.5 %psum.15 = f32[128,32]{1,0:T(8,128)S(1)} all-reduce(f32[128,32]{1,0:T(8,128)S(1)} %select_select_fusion), channel_id=1, replica_groups=mesh['dp'=32,'table'=16] {'table'}, use_global_device_ids=true, to_apply=%region_7.8 | all-reduce | flops 4096 | bytes 32768 | tf_op jit(solution)/shard_map/psum | solution.py:74
  287.1 28.6 %scatter_custom_fusion = bf16[16384]{0:T(1024)(128)(2,1)S(1)} fusion(s32[4096]{0:T(1024)S(1)} %reshape.49, bf16[4096]{0:T(1024)(128)(2,1)S(1)} %reshape.51, bf16[]{:T(256)} %constant.110.clone.1), kind=kCustom, calls=%fused_computation.33 | custom fusion | bytes 32770
  317.2 10.4 %all-to-all-start = ((bf16[128,16,256]{2,0,1:T(8,128)(2,1)}), bf16[128,16,256]{2,0,1:T(8,128)(2,1)S(1)}, u32[]{:S(2)}, u32[]{:S(2)}) async-start(bf16[128,16,256]{2,0,1:T(8,128)(2,1)} %bitcast.29), calls=%async_computation | async-start | bytes 2097152 | tf_op jit(solution)/shard_map/all_to_all | solution.py:53
  329.1 31.6 %all-to-all-done = bf16[128,16,256]{2,0,1:T(8,128)(2,1)S(1)} async-done(((bf16[128,16,256]{2,0,1:T(8,128)(2,1)}), bf16[128,16,256]{2,0,1:T(8,128)(2,1)S(1)}, u32[]{:S(2)}, u32[]{:S(2)}) %all-to-all-start) | async-done | bytes 1048608 | tf_op jit(solution)/shard_map/all_to_all | solution.py:53
  361.5 1.9 fusion
  363.5 2.5 copy.29
  370.1 97.7 %all-reduce.2.cloned.1.call-done = bf16[128,4096]{1,0:T(8,128)(2,1)} async-done(((bf16[128,4096]{1,0:T(8,128)(2,1)}), bf16[128,4096]{1,0:T(8,128)(2,1)}) %all-reduce.2.cloned.1.call-update) | async-done | bytes 1048592 | tf_op jit(solution)/shard_map/psum | solution.py:76
  467.8 2.8 convert_element_type.53
  470.5 102.8 %reduce-scatter.7.cloned.1.call-done = bf16[128,256]{1,0:T(8,128)(2,1)} async-done(((bf16[4096,256]{1,0:T(8,128)(2,1)}), bf16[128,256]{1,0:T(8,128)(2,1)}) %reduce-scatter.7.cloned.1.call-update) | async-done | bytes 65552
  575.0 72.0 %reduce-scatter.5.cloned.1.call-done = bf16[128,256]{1,0:T(8,128)(2,1)} async-done(((bf16[128,4096]{1,0:T(8,128)(2,1)}), bf16[128,256]{1,0:T(8,128)(2,1)}) %reduce-scatter.5.cloned.1.call-update) | async-done | bytes 65552 | tf_op jit(solution)/shard_map/reduce_scatter | solution.py:88
  (81 shorter events, 29.4 us)
Async XLA Ops:
  7.2 199.8 %copy-start = (bf16[128,4096]{1,0:T(8,128)(2,1)S(1)}, bf16[128,4096]{1,0:T(8,128)(2,1)}, u32[]{:S(2)}) copy-start(bf16[128,4096]{1,0:T(8,128)(2,1)} %param.8) | copy-start | bytes 3145732
  7.2 137.4 %copy-start.2 = (bf16[128,256]{1,0:T(8,128)(2,1)S(1)}, bf16[128,256]{1,0:T(8,128)(2,1)}, u32[]{:S(2)}) copy-start(bf16[128,256]{1,0:T(8,128)(2,1)} %param.11) | copy-start | bytes 196612
  7.2 79.6 %all-gather.3.cloned.1.call-start = ((), (), s32[]{:S(2)}) async-start(), calls=%async_computation.3 | async-start | bytes 1114112 | tf_op jit(solution)/shard_map/all_gather | solution.py:46
  7.9 136.5 %all-gather.5.cloned.1.call-start = ((), (), s32[]{:S(2)}) async-start(), calls=%async_computation.4 | async-start | bytes 2162688 | tf_op jit(solution)/shard_map/all_gather | solution.py:47
  147.0 8.5 %collective-permute-start = (bf16[128,256]{1,0:T(8,128)(2,1)S(1)}, bf16[128,256]{1,0:T(8,128)(2,1)S(1)}, u32[]{:S(2)}, u32[]{:S(2)}) collective-permute-start(bf16[128,256]{1,0:T(8,128)(2,1)S(1)} %get-tuple-element.26), channel_id=1, source_target_pairs={{0,1},{1,2},{2,3},{3,4},{4,5},{5,6},{6,7},{7,8},{8,9},{9,10},{10,1... | collective-permute-start | bytes 196616 | tf_op jit(solution)/shard_map/ppermute | solution.py:16
  150.4 6.9 %collective-permute-start.1 = (bf16[128,256]{1,0:T(8,128)(2,1)S(1)}, bf16[128,256]{1,0:T(8,128)(2,1)S(1)}, u32[]{:S(2)}, u32[]{:S(2)}) collective-permute-start(bf16[128,256]{1,0:T(8,128)(2,1)S(1)} %get-tuple-element.26), channel_id=1, source_target_pairs={{0,15},{1,0},{2,1},{3,2},{4,3},{5,4},{6,5},{7,6},{8,7},{9,8},{10,9... | collective-permute-start | bytes 196616 | tf_op jit(solution)/shard_map/ppermute | solution.py:21
  155.4 7.4 %collective-permute-start.2 = (bf16[128,256]{1,0:T(8,128)(2,1)S(1)}, bf16[128,256]{1,0:T(8,128)(2,1)S(1)}, u32[]{:S(2)}, u32[]{:S(2)}) collective-permute-start(bf16[128,256]{1,0:T(8,128)(2,1)S(1)} %collective-permute-done), channel_id=1, source_target_pairs={{0,1},{1,2},{2,3},{3,4},{4,5},{5,6},{6,7},{7,8},{8,9},{9,10},{10,1... | collective-permute-start | bytes 196616 | tf_op jit(solution)/shard_map/ppermute | solution.py:16
  157.3 7.4 %collective-permute-start.3 = (bf16[128,256]{1,0:T(8,128)(2,1)S(1)}, bf16[128,256]{1,0:T(8,128)(2,1)S(1)}, u32[]{:S(2)}, u32[]{:S(2)}) collective-permute-start(bf16[128,256]{1,0:T(8,128)(2,1)S(1)} %collective-permute-done.1), channel_id=1, source_target_pairs={{0,15},{1,0},{2,1},{3,2},{4,3},{5,4},{6,5},{7,6},{8,7},{9,8},{10,9... | collective-permute-start | bytes 196616 | tf_op jit(solution)/shard_map/ppermute | solution.py:21
  162.8 7.4 %collective-permute-start.4 = (bf16[128,256]{1,0:T(8,128)(2,1)S(1)}, bf16[128,256]{1,0:T(8,128)(2,1)S(1)}, u32[]{:S(2)}, u32[]{:S(2)}) collective-permute-start(bf16[128,256]{1,0:T(8,128)(2,1)S(1)} %collective-permute-done.2), channel_id=1, source_target_pairs={{0,1},{1,2},{2,3},{3,4},{4,5},{5,6},{6,7},{7,8},{8,9},{9,10},{10,1... | collective-permute-start | bytes 196616 | tf_op jit(solution)/shard_map/ppermute | solution.py:16
  164.7 7.4 %collective-permute-start.5 = (bf16[128,256]{1,0:T(8,128)(2,1)S(1)}, bf16[128,256]{1,0:T(8,128)(2,1)S(1)}, u32[]{:S(2)}, u32[]{:S(2)}) collective-permute-start(bf16[128,256]{1,0:T(8,128)(2,1)S(1)} %collective-permute-done.3), channel_id=1, source_target_pairs={{0,15},{1,0},{2,1},{3,2},{4,3},{5,4},{6,5},{7,6},{8,7},{9,8},{10,9... | collective-permute-start | bytes 196616 | tf_op jit(solution)/shard_map/ppermute | solution.py:21
  170.1 7.4 %collective-permute-start.6 = (bf16[128,256]{1,0:T(8,128)(2,1)S(1)}, bf16[128,256]{1,0:T(8,128)(2,1)S(1)}, u32[]{:S(2)}, u32[]{:S(2)}) collective-permute-start(bf16[128,256]{1,0:T(8,128)(2,1)S(1)} %collective-permute-done.4), channel_id=1, source_target_pairs={{0,1},{1,2},{2,3},{3,4},{4,5},{5,6},{6,7},{7,8},{8,9},{9,10},{10,1... | collective-permute-start | bytes 196616 | tf_op jit(solution)/shard_map/ppermute | solution.py:16
  172.1 7.4 %collective-permute-start.7 = (bf16[128,256]{1,0:T(8,128)(2,1)S(1)}, bf16[128,256]{1,0:T(8,128)(2,1)S(1)}, u32[]{:S(2)}, u32[]{:S(2)}) collective-permute-start(bf16[128,256]{1,0:T(8,128)(2,1)S(1)} %collective-permute-done.5), channel_id=1, source_target_pairs={{0,15},{1,0},{2,1},{3,2},{4,3},{5,4},{6,5},{7,6},{8,7},{9,8},{10,9... | collective-permute-start | bytes 196616 | tf_op jit(solution)/shard_map/ppermute | solution.py:21
  177.5 7.4 %collective-permute-start.8 = (bf16[128,256]{1,0:T(8,128)(2,1)S(1)}, bf16[128,256]{1,0:T(8,128)(2,1)S(1)}, u32[]{:S(2)}, u32[]{:S(2)}) collective-permute-start(bf16[128,256]{1,0:T(8,128)(2,1)S(1)} %collective-permute-done.6), channel_id=1, source_target_pairs={{0,1},{1,2},{2,3},{3,4},{4,5},{5,6},{6,7},{7,8},{8,9},{9,10},{10,1... | collective-permute-start | bytes 196616 | tf_op jit(solution)/shard_map/ppermute | solution.py:16
  179.4 7.4 %collective-permute-start.9 = (bf16[128,256]{1,0:T(8,128)(2,1)S(1)}, bf16[128,256]{1,0:T(8,128)(2,1)S(1)}, u32[]{:S(2)}, u32[]{:S(2)}) collective-permute-start(bf16[128,256]{1,0:T(8,128)(2,1)S(1)} %collective-permute-done.7), channel_id=1, source_target_pairs={{0,15},{1,0},{2,1},{3,2},{4,3},{5,4},{6,5},{7,6},{8,7},{9,8},{10,9... | collective-permute-start | bytes 196616 | tf_op jit(solution)/shard_map/ppermute | solution.py:21
  184.8 7.4 %collective-permute-start.10 = (bf16[128,256]{1,0:T(8,128)(2,1)S(1)}, bf16[128,256]{1,0:T(8,128)(2,1)S(1)}, u32[]{:S(2)}, u32[]{:S(2)}) collective-permute-start(bf16[128,256]{1,0:T(8,128)(2,1)S(1)} %collective-permute-done.8), channel_id=1, source_target_pairs={{0,1},{1,2},{2,3},{3,4},{4,5},{5,6},{6,7},{7,8},{8,9},{9,10},{10,1... | collective-permute-start | bytes 196616 | tf_op jit(solution)/shard_map/ppermute | solution.py:16
  186.8 7.4 %collective-permute-start.11 = (bf16[128,256]{1,0:T(8,128)(2,1)S(1)}, bf16[128,256]{1,0:T(8,128)(2,1)S(1)}, u32[]{:S(2)}, u32[]{:S(2)}) collective-permute-start(bf16[128,256]{1,0:T(8,128)(2,1)S(1)} %collective-permute-done.9), channel_id=1, source_target_pairs={{0,15},{1,0},{2,1},{3,2},{4,3},{5,4},{6,5},{7,6},{8,7},{9,8},{10,9... | collective-permute-start | bytes 196616 | tf_op jit(solution)/shard_map/ppermute | solution.py:21
  192.2 7.4 %collective-permute-start.12 = (bf16[128,256]{1,0:T(8,128)(2,1)S(1)}, bf16[128,256]{1,0:T(8,128)(2,1)S(1)}, u32[]{:S(2)}, u32[]{:S(2)}) collective-permute-start(bf16[128,256]{1,0:T(8,128)(2,1)S(1)} %collective-permute-done.10), channel_id=1, source_target_pairs={{0,1},{1,2},{2,3},{3,4},{4,5},{5,6},{6,7},{7,8},{8,9},{9,10},{10,1... | collective-permute-start | bytes 196616 | tf_op jit(solution)/shard_map/ppermute | solution.py:16
  194.1 7.4 %collective-permute-start.13 = (bf16[128,256]{1,0:T(8,128)(2,1)S(1)}, bf16[128,256]{1,0:T(8,128)(2,1)S(1)}, u32[]{:S(2)}, u32[]{:S(2)}) collective-permute-start(bf16[128,256]{1,0:T(8,128)(2,1)S(1)} %collective-permute-done.11), channel_id=1, source_target_pairs={{0,15},{1,0},{2,1},{3,2},{4,3},{5,4},{6,5},{7,6},{8,7},{9,8},{10,9... | collective-permute-start | bytes 196616 | tf_op jit(solution)/shard_map/ppermute | solution.py:21
  199.6 7.4 %collective-permute-start.14 = (bf16[128,256]{1,0:T(8,128)(2,1)S(1)}, bf16[128,256]{1,0:T(8,128)(2,1)S(1)}, u32[]{:S(2)}, u32[]{:S(2)}) collective-permute-start(bf16[128,256]{1,0:T(8,128)(2,1)S(1)} %collective-permute-done.12), channel_id=1, source_target_pairs={{0,1},{1,2},{2,3},{3,4},{4,5},{5,6},{6,7},{7,8},{8,9},{9,10},{10,1... | collective-permute-start | bytes 196616 | tf_op jit(solution)/shard_map/ppermute | solution.py:16
  317.2 43.5 %all-to-all-start = ((bf16[128,16,256]{2,0,1:T(8,128)(2,1)}), bf16[128,16,256]{2,0,1:T(8,128)(2,1)S(1)}, u32[]{:S(2)}, u32[]{:S(2)}) async-start(bf16[128,16,256]{2,0,1:T(8,128)(2,1)} %bitcast.29), calls=%async_computation | async-start | bytes 2097152 | tf_op jit(solution)/shard_map/all_to_all | solution.py:53
  327.6 140.2 %all-reduce.2.cloned.1.call-start = ((), (), s32[]{:S(2)}) async-start(), calls=%async_computation.6 | async-start | bytes 2097152 | tf_op jit(solution)/shard_map/psum | solution.py:76
  329.1 244.2 %reduce-scatter.7.cloned.1.call-start = ((), (), s32[]{:S(2)}) async-start(), calls=%async_computation.7 | async-start | bytes 2162688
  366.0 1.6 copy-start.1
  366.0 281.0 %reduce-scatter.5.cloned.1.call-start = ((), (), s32[]{:S(2)}) async-start(), calls=%async_computation.5 | async-start | bytes 1114112 | tf_op jit(solution)/shard_map/reduce_scatter | solution.py:88
Sparse Core Ops, SparseCore 0:
  10.0 76.6 all-gather.2
  89.9 54.5 all-gather.4
  331.6 136.1 all-reduce.1
  472.7 100.5 reduce-scatter.6
  576.8 70.1 reduce-scatter.4
